TPU v7x, 512 devices: a whole 4x8x8 slice. The times are simulated.
512 devices in a mesh: dp: 4 (over x), row: 32 (over y, z_hi, core), col: 4 (over z_lo).
Axes of the slice: x: 4, y: 8, z: 8 (z_hi: 2, z_lo: 4; z = z_hi * 4 + z_lo), core: 2. Of those that a mesh axis runs over, the one named last changes fastest.
Arguments:
- tokens: bfloat16 [2048, 8192], P('dp', ('row', 'col')), may hold values from -6 to 6
- hidden_grad: bfloat16 [2048, 6656], P(('dp', 'row'), 'col'), may hold values from -6 to 6
- gate_weight: bfloat16 [8192, 6656], P('row', 'col'), may hold values from -0.0625 to 0.0625
- up_weight: bfloat16 [8192, 6656], P('row', 'col'), may hold values from -0.0625 to 0.0625
Outputs:
- input_grad: bfloat16 [2048, 8192], P('dp', ('row', 'col'))
- gate_grad: bfloat16 [8192, 6656], P('row', 'col')
- up_grad: bfloat16 [8192, 6656], P('row', 'col')
All inputs are finite; a program needn't handle non-finite values.
Results may differ from a plain program's by a relative error of at most 0.022.
Values may be sent and summed in bfloat16 or wider, within the bound.
A program may use at most 64 MiB of HBM per device.

v0:
```python
import jax
import jax.numpy as jnp
from jax import lax
from jax.sharding import PartitionSpec as P


def contract_rows(left, right):
    return lax.dot_general(
        left, right, (((0,), (0,)), ((), ())), preferred_element_type=jnp.float32
    )


def contract_cols(left, right):
    return lax.dot_general(
        left, right, (((1,), (1,)), ((), ())), preferred_element_type=jnp.float32
    )


def body(tokens, hidden_grad, gate_weight, up_weight):
    panel = lax.all_gather(tokens, "col", axis=1, tiled=True)
    width = gate_weight.shape[1]
    shares = lax.psum_scatter(
        jnp.concatenate(
            [
                jnp.dot(panel, gate_weight, preferred_element_type=jnp.float32),
                jnp.dot(panel, up_weight, preferred_element_type=jnp.float32),
            ],
            axis=1,
        ).astype(jnp.bfloat16),
        "row",
        scatter_dimension=0,
        tiled=True,
    ).astype(jnp.float32)
    gate = shares[:, :width]
    up = shares[:, width:]
    sigma = jax.nn.sigmoid(gate)
    upstream = hidden_grad.astype(jnp.float32)
    gate_act = (upstream * up * sigma * (1.0 + gate * (1.0 - sigma))).astype(jnp.bfloat16)
    up_act = (upstream * gate * sigma).astype(jnp.bfloat16)
    gate_panel, up_panel = (
        lax.all_gather(gate_act, "row", axis=0, tiled=True),
        lax.all_gather(up_act, "row", axis=0, tiled=True),
    )
    input_share = lax.psum_scatter(
        (contract_cols(gate_weight, gate_panel) + contract_cols(up_weight, up_panel)).astype(
            jnp.bfloat16
        ),
        "col",
        scatter_dimension=0,
        tiled=True,
    ).astype(jnp.float32)
    input_grad = input_share.T.astype(jnp.bfloat16)
    gate_local = contract_rows(panel, gate_panel)
    up_local = contract_rows(panel, up_panel)
    gate_sum, up_sum = (
        lax.psum(gate_local.astype(jnp.bfloat16), "dp").astype(jnp.float32),
        lax.psum(up_local.astype(jnp.bfloat16), "dp").astype(jnp.float32),
    )
    return (input_grad, gate_sum.astype(jnp.bfloat16), up_sum.astype(jnp.bfloat16))


def solution(mesh):
    return jax.shard_map(
        body,
        mesh=mesh,
        in_specs=(
            P("dp", ("row", "col")),
            P(("dp", "row"), "col"),
            P("row", "col"),
            P("row", "col"),
        ),
        out_specs=(P("dp", ("row", "col")), P("row", "col"), P("row", "col")),
        check_vma=False,
    )
```

profile of v0, /device:TPU:1, one launch (start us, length us, event | category | flops | bytes accessed | tf_op | source)
XLA Modules:
  0.0 453.1 jit_solution(16732908509172800166)
XLA Ops:
  7.2 0.0 reduce-scatter.5.cloned.1.call-start
  7.2 15.9 %all_gather.9 = bf16[512,256]{0,1:T(8,128)(2,1)S(1)} all-gather(bf16[512,64]{0,1:T(8,128)(2,1)} %param.4), channel_id=1, replica_groups=mesh['dp'=4,'row'=32,'col'=4] {'col'}, dimensions={1}, use_global_device_ids=true | all-gather | bytes 327680 | tf_op jit(solution)/shard_map/all_gather | solution.py:20
  23.2 1.8 convolution_convert_fusion
  25.0 0.7 convolution_convert_fusion.1
  25.7 1.9 pad_maximum_fusion
  27.6 0.0 all-gather.3.cloned.1.call-start
  27.7 145.1 %reduce-scatter.5.cloned.1.call-done = bf16[16,3328]{1,0:T(8,128)(2,1)} async-done(((bf16[512,3328]{1,0:T(8,128)(2,1)}), bf16[16,3328]{1,0:T(8,128)(2,1)}) %reduce-scatter.5.cloned.1.call-update) | async-done | bytes 106512 | tf_op jit(solution)/shard_map/reduce_scatter | solution.py:22
  172.8 0.9 convert_element_type.41
  173.7 0.7 fusion.8
  174.4 0.0 all-gather.5.cloned.1.call-start
  174.5 0.7 all-gather.5.cloned.1.call-update
  175.2 0.0 all-reduce.3.cloned.1.call-start
  175.2 94.0 %all-gather.3.cloned.1.call-done = bf16[512,1664]{1,0:T(8,128)(2,1)} async-done(((bf16[16,1664]{1,0:T(8,128)(2,1)}), bf16[512,1664]{1,0:T(8,128)(2,1)}) %all-gather.3.cloned.1.call-update) | async-done | bytes 1703952 | tf_op jit(solution)/shard_map/all_gather | solution.py:41
  269.2 3.0 fusion
  272.2 86.0 %all-gather.5.cloned.1.call-done = bf16[512,1664]{1,0:T(8,128)(2,1)} async-done(((bf16[16,1664]{1,0:T(8,128)(2,1)}), bf16[512,1664]{1,0:T(8,128)(2,1)}) %all-gather.5.cloned.1.call-update) | async-done | bytes 1703952 | tf_op jit(solution)/shard_map/all_gather | solution.py:42
  358.2 3.0 fusion.1
  361.3 0.0 reduce-scatter.7.cloned.1.call-start
  361.3 2.3 fusion.9
  363.6 1.4 fusion.3
  365.0 1.8 copy.13
  366.8 50.5 %all-reduce.3.cloned.1.call-done = (bf16[256,1664]{0,1:T(8,128)(2,1)}, bf16[256,1664]{0,1:T(8,128)(2,1)}) async-done(((bf16[256,1664]{0,1:T(8,128)(2,1)}, bf16[256,1664]{0,1:T(8,128)(2,1)}), (bf16[256,1664]{0,1:T(8,128)(2,1)}, bf16[256,1664]{0,1:T(8,128)(2,1)})) %all-reduce.3.cloned.1.call-update) | async-done | bytes 1703952 | tf_op jit(solution)/shard_map/psum | solution.py:56
  417.4 2.3 copy.11
  419.6 1.3 copy.12
  421.0 25.6 %reduce-scatter.7.cloned.1.call-done = bf16[64,512]{1,0:T(8,128)(2,1)} async-done(((bf16[256,512]{1,0:T(8,128)(2,1)}), bf16[64,512]{1,0:T(8,128)(2,1)}) %reduce-scatter.7.cloned.1.call-update) | async-done | bytes 65552
  (14 shorter events, 0.1 us)
Async XLA Ops:
  7.2 17.8 %copy-start = (bf16[256,1664]{1,0:T(8,128)(2,1)S(1)}, bf16[256,1664]{1,0:T(8,128)(2,1)}, u32[]{:S(2)}) copy-start(bf16[256,1664]{1,0:T(8,128)(2,1)} %param.6) | copy-start | bytes 2555908
  7.2 165.6 %reduce-scatter.5.cloned.1.call-start = ((), (), s32[]{:S(2)}) async-start(), calls=%async_computation.2 | async-start | bytes 3514368 | tf_op jit(solution)/shard_map/reduce_scatter | solution.py:22
  27.6 146.1 %copy-start.4 = (bf16[16,1664]{1,0:T(8,128)(2,1)S(1)}, bf16[16,1664]{1,0:T(8,128)(2,1)}, u32[]{:S(2)}) copy-start(bf16[16,1664]{1,0:T(8,128)(2,1)} %param.5) | copy-start | bytes 159748
  27.6 241.5 %all-gather.3.cloned.1.call-start = ((), (), s32[]{:S(2)}) async-start(), calls=%async_computation.3 | async-start | bytes 1757184 | tf_op jit(solution)/shard_map/all_gather | solution.py:41
  174.4 183.8 %all-gather.5.cloned.1.call-start = ((), (), s32[]{:S(2)}) async-start(), calls=%async_computation.4 | async-start | bytes 1757184 | tf_op jit(solution)/shard_map/all_gather | solution.py:42
  175.2 242.2 %all-reduce.3.cloned.1.call-start = ((), (), s32[]{:S(2)}) async-start(), calls=%async_computation.6 | async-start | bytes 3407872 | tf_op jit(solution)/shard_map/psum | solution.py:56
  361.2 2.4 copy-start.1
  361.3 2.4 copy-start.2
  361.3 85.3 %reduce-scatter.7.cloned.1.call-start = ((), (), s32[]{:S(2)}) async-start(), calls=%async_computation.5 | async-start | bytes 327680
  417.4 2.3 copy-start.3
Sparse Core Ops, SparseCore 0:
  27.8 144.9 reduce-scatter.4
  176.7 92.4 all-gather.2
  273.0 85.1 all-gather.4
  361.4 55.9 all-reduce.2
  420.6 25.9 reduce-scatter.6
where the time goes:
time: 455 us; the launch traced here: 453 us
  waiting for transfers between devices  402 us (88%)
  blocking collectives  15.9 us (3%)
  between operations  13.9 us (3%)
  matrix products  12.2 us (3%)
  local copies, waits for them, and re-layouts  5.43 us (1%)
    reduce_scatter x1, waiting for transfers between devices, body(): lax.psum_scatter(jnp.concatenate([jnp.dot(panel, gate_weight, preferred_e...  145 us
    all_gather x1, waiting for transfers between devices, body(): lax.all_gather(gate_act, 'row', axis=0, tiled=True)  94 us
    all_gather x1, waiting for transfers between devices, body(): lax.all_gather(up_act, 'row', axis=0, tiled=True)  86 us
    psum x1, waiting for transfers between devices, body(): lax.psum(gate_local.astype(jnp.bfloat16), 'dp').astype(jnp.float32)  50.5 us
    unnamed x6, waiting for transfers between devices  26.3 us
    all_gather x1, blocking collectives, body(): panel = lax.all_gather(tokens, 'col', axis=1, tiled=True)  15.9 us
  transfers between devices with their start and end apart: 5, of which 5 were waited for; matrix products, arithmetic and copies ran while one was open for 3% of the time, Pallas kernels for 0%

commit v1 on v0

v1 whole, which is shorter than its diff:
```python
import jax
import jax.numpy as jnp
from jax import lax
from jax.experimental import pallas as pl
from jax.experimental.pallas import tpu as pltpu
from jax.sharding import PartitionSpec as P

MESH = pl.DeviceIdType.MESH
F32 = jnp.float32
BF16 = jnp.bfloat16
NY, NX, NC = 8, 4, 4


def remote(src, dst, send, recv, target):
    copy = pltpu.make_async_remote_copy(
        src_ref=src,
        dst_ref=dst,
        send_sem=send,
        recv_sem=recv,
        device_id=target,
        device_id_type=MESH,
    )
    copy.start()
    return copy


def greet(targets):
    barrier = pltpu.get_barrier_semaphore()
    for target in targets:
        pl.semaphore_signal(barrier, inc=1, device_id=target, device_id_type=MESH)
    pl.semaphore_wait(barrier, len(targets))


def vmem():
    return pl.BlockSpec(memory_space=pltpu.VMEM)


def params(collective_id):
    return pltpu.CompilerParams(collective_id=collective_id, has_side_effects=True)


def gather_kernel(mine_ref, all_ref, local_sem, send_sem, recv_sem):
    col = lax.axis_index("col")
    peers = [{"col": lax.rem(col + o, NC)} for o in range(1, NC)]
    greet(peers)
    copies = [
        remote(mine_ref, all_ref.at[col], send_sem.at[o], recv_sem.at[o], peers[o])
        for o in range(NC - 1)
    ]
    own = pltpu.make_async_copy(mine_ref, all_ref.at[col], local_sem)
    own.start()
    own.wait()
    for copy in copies:
        copy.wait()


def gather_tokens(block):
    rows, tokens = block.shape
    return pl.pallas_call(
        gather_kernel,
        out_shape=jax.ShapeDtypeStruct((NC, rows, tokens), BF16),
        in_specs=[vmem()],
        out_specs=vmem(),
        scratch_shapes=[
            pltpu.SemaphoreType.DMA,
            pltpu.SemaphoreType.DMA((NC - 1,)),
            pltpu.SemaphoreType.DMA((NC - 1,)),
        ],
        compiler_params=params(0),
        name="gather_tokens",
    )(block)


def row_kernel(
    gate_ref, up_ref, hidden_ref, gate_out, up_out,
    core_in, ring_out, ring_in, own, pair_out, pair_in,
    core_send, core_recv, ring_send, ring_recv, pair_send, pair_recv,
    swap_send, swap_recv, turn_send, turn_recv, fwd_send, fwd_recv,
):
    row = lax.axis_index("row")
    y = lax.div(row, 4)
    core = lax.rem(row, 2)
    zh = lax.rem(lax.div(row, 2), 2)
    low = lax.rem(row, 4)
    ahead = {"row": lax.rem(y + 1, NY) * 4 + low}
    behind = {"row": lax.rem(y + NY - 1, NY) * 4 + low}
    partner = {"row": y * 4 + zh * 2 + (1 - core)}
    pair = {"row": y * 4 + (1 - zh) * 2 + core}
    greet([ahead, behind, partner, pair])

    ins = (gate_ref, up_ref)
    outs = (gate_out, up_out)
    nexts = (ahead, behind)
    zhs = (1 - zh, zh)

    def chunk(way, s):
        return lax.rem(y + NY - 1 - s, NY) if way == 0 else lax.rem(y + 1 + s, NY)

    started = []
    core_copies = {}
    for s in range(NY):
        for way in range(2):
            core_copies[way, s] = remote(
                ins[way].at[chunk(way, s), :, 1 - core],
                core_in.at[way, s],
                core_send.at[way, s],
                core_recv.at[way, s],
                partner,
            )
    ring_copies = {}
    pair_copies = []
    for s in range(NY):
        for way in range(2):
            core_copies[way, s].wait_recv()
        for j in range(2):
            for way in range(2):
                total = (
                    ins[way][chunk(way, s), zhs[j], core].astype(F32)
                    + core_in[way, s, zhs[j]].astype(F32)
                )
                if s > 0:
                    ring_copies[way, j, s - 1].wait_recv()
                    total = total + ring_in[way, j, s - 1].astype(F32)
                if s < NY - 1:
                    ring_out[way, j, s] = total.astype(BF16)
                    ring_copies[way, j, s] = remote(
                        ring_out.at[way, j, s],
                        ring_in.at[way, j, s],
                        ring_send.at[way, j, s],
                        ring_recv.at[way, j, s],
                        nexts[way],
                    )
                elif j == 0:
                    pair_out[way] = total.astype(BF16)
                    pair_copies.append(
                        remote(
                            pair_out.at[way],
                            pair_in.at[way],
                            pair_send.at[way],
                            pair_recv.at[way],
                            pair,
                        )
                    )
                else:
                    own[way] = total
    for copy in pair_copies:
        copy.wait_recv()
    gate = own[0] + pair_in[0].astype(F32)
    up = own[1] + pair_in[1].astype(F32)
    sigma = jax.nn.sigmoid(gate)
    upstream = hidden_ref[...].astype(F32)
    gate_out[y, zh, core] = (upstream * up * sigma * (1.0 + gate * (1.0 - sigma))).astype(BF16)
    up_out[y, zh, core] = (upstream * gate * sigma).astype(BF16)

    def place(way, j, s):
        at = lax.rem(y + NY - s, NY) if way == 0 else lax.rem(y + s, NY)
        return outs[way].at[at, zhs[j], core]

    swap_copies = [
        remote(place(way, 1, 0), place(way, 1, 0), swap_send.at[way], swap_recv.at[way], pair)
        for way in range(2)
    ]
    turn_copies = {}
    fwd_copies = {}

    def pass_on(way, j, s):
        here = place(way, j, s)
        if s < NY - 1:
            turn_copies[way, j, s] = remote(
                here, here, turn_send.at[way, j, s], turn_recv.at[way, j, s], nexts[way]
            )
        fwd_copies[way, j, s] = remote(
            here, here, fwd_send.at[way, j, s], fwd_recv.at[way, j, s], partner
        )

    late = 4
    for s in range(NY + late):
        if s < NY:
            for way in range(2):
                if s > 0:
                    turn_copies[way, 1, s - 1].wait_recv()
                pass_on(way, 1, s)
        if s >= late:
            for way in range(2):
                if s == late:
                    swap_copies[way].wait_recv()
                else:
                    turn_copies[way, 0, s - late - 1].wait_recv()
                pass_on(way, 0, s - late)
    for copy in fwd_copies.values():
        copy.wait_recv()
    for group in (core_copies, ring_copies, turn_copies, fwd_copies):
        started.extend(group.values())
    for copy in started + pair_copies + swap_copies:
        copy.wait_send()


def row_exchange(gate, up, hidden):
    rows, width = hidden.shape
    shape = (NY, 2, 2, rows, width)
    dma = pltpu.SemaphoreType.DMA
    gate_act, up_act = pl.pallas_call(
        row_kernel,
        out_shape=[jax.ShapeDtypeStruct(shape, BF16)] * 2,
        in_specs=[vmem()] * 3,
        out_specs=[vmem()] * 2,
        scratch_shapes=[
            pltpu.VMEM((2, NY, 2, rows, width), BF16),
            pltpu.VMEM((2, 2, NY - 1, rows, width), BF16),
            pltpu.VMEM((2, 2, NY - 1, rows, width), BF16),
            pltpu.VMEM((2, rows, width), F32),
            pltpu.VMEM((2, rows, width), BF16),
            pltpu.VMEM((2, rows, width), BF16),
            dma((2, NY)),
            dma((2, NY)),
            dma((2, 2, NY - 1)),
            dma((2, 2, NY - 1)),
            dma((2,)),
            dma((2,)),
            dma((2,)),
            dma((2,)),
            dma((2, 2, NY - 1)),
            dma((2, 2, NY - 1)),
            dma((2, 2, NY)),
            dma((2, 2, NY)),
        ],
        compiler_params=params(1),
        name="row_exchange",
    )(gate.reshape(shape), up.reshape(shape), hidden)
    return gate_act.reshape(-1, width), up_act.reshape(-1, width)


def sum_kernel(
    gate_ref, up_ref, input_ref, gate_out, up_out, input_out,
    ring_out, ring_in, peer_in,
    ring_send, ring_recv, turn_send, turn_recv, peer_send, peer_recv,
):
    dp = lax.axis_index("dp")
    col = lax.axis_index("col")
    nexts = ({"dp": lax.rem(dp + 1, NX)}, {"dp": lax.rem(dp + NX - 1, NX)})
    peers = [{"col": lax.rem(col + o, NC)} for o in range(1, NC)]
    greet([*nexts, *peers])
    ins = (gate_ref, up_ref)
    outs = (gate_out, up_out)

    def chunk(way, s):
        return lax.rem(dp + NX - 1 - s, NX) if way == 0 else lax.rem(dp + 1 + s, NX)

    ring_copies = {}
    turn_copies = {}
    peer_copies = []
    for s in range(NX):
        for j in range(2):
            for way in range(2):
                here = chunk(way, s)
                if s == 0:
                    ring_copies[way, j, s] = remote(
                        ins[way].at[here, j],
                        ring_in.at[way, j, s],
                        ring_send.at[way, j, s],
                        ring_recv.at[way, j, s],
                        nexts[way],
                    )
                    continue
                ring_copies[way, j, s - 1].wait_recv()
                total = ins[way][here, j].astype(F32) + ring_in[way, j, s - 1].astype(F32)
                if s < NX - 1:
                    ring_out[way, j, s - 1] = total.astype(BF16)
                    ring_copies[way, j, s] = remote(
                        ring_out.at[way, j, s - 1],
                        ring_in.at[way, j, s],
                        ring_send.at[way, j, s],
                        ring_recv.at[way, j, s],
                        nexts[way],
                    )
                else:
                    outs[way][here, j] = total.astype(BF16)
                    turn_copies[way, j, 0] = remote(
                        outs[way].at[here, j],
                        outs[way].at[here, j],
                        turn_send.at[way, j, 0],
                        turn_recv.at[way, j, 0],
                        nexts[way],
                    )
        if s == 0:
            for o in range(NC - 1):
                peer_copies.append(
                    remote(
                        input_ref.at[lax.rem(col + o + 1, NC)],
                        peer_in.at[o],
                        peer_send.at[o],
                        peer_recv.at[o],
                        peers[o],
                    )
                )
    for s in range(1, NX - 1):
        for j in range(2):
            for way in range(2):
                turn_copies[way, j, s - 1].wait_recv()
                at = lax.rem(dp + NX - s, NX) if way == 0 else lax.rem(dp + s, NX)
                turn_copies[way, j, s] = remote(
                    outs[way].at[at, j],
                    outs[way].at[at, j],
                    turn_send.at[way, j, s],
                    turn_recv.at[way, j, s],
                    nexts[way],
                )
    total = input_ref[col].astype(F32)
    for o in range(NC - 1):
        peer_copies[o].wait_recv()
        total = total + peer_in[o].astype(F32)
    input_out[...] = total.astype(BF16)
    for j in range(2):
        for way in range(2):
            turn_copies[way, j, NX - 2].wait_recv()
    for copy in [*ring_copies.values(), *turn_copies.values(), *peer_copies]:
        copy.wait_send()


def sum_grads(gate, up, share):
    features, width = gate.shape
    tokens = share.shape[1]
    half = features // NX // 2
    shape = (NX, 2, half, width)
    rows = features // NC
    dma = pltpu.SemaphoreType.DMA
    gate_sum, up_sum, input_sum = pl.pallas_call(
        sum_kernel,
        out_shape=[jax.ShapeDtypeStruct(shape, BF16)] * 2
        + [jax.ShapeDtypeStruct((rows, tokens), BF16)],
        in_specs=[vmem()] * 3,
        out_specs=[vmem()] * 3,
        scratch_shapes=[
            pltpu.VMEM((2, 2, NX - 2, half, width), BF16),
            pltpu.VMEM((2, 2, NX - 1, half, width), BF16),
            pltpu.VMEM((NC - 1, rows, tokens), BF16),
            dma((2, 2, NX - 1)),
            dma((2, 2, NX - 1)),
            dma((2, 2, NX - 1)),
            dma((2, 2, NX - 1)),
            dma((NC - 1,)),
            dma((NC - 1,)),
        ],
        compiler_params=params(2),
        name="sum_grads",
    )(gate.reshape(shape), up.reshape(shape), share.reshape(NC, rows, tokens))
    return gate_sum.reshape(features, width), up_sum.reshape(features, width), input_sum


def contract_rows(left, right):
    return lax.dot_general(left, right, (((0,), (0,)), ((), ())), preferred_element_type=F32)


def contract_cols(left, right):
    return lax.dot_general(left, right, (((1,), (1,)), ((), ())), preferred_element_type=F32)


def body(tokens, hidden_grad, gate_weight, up_weight):
    features = gate_weight.shape[0]
    panel_t = gather_tokens(tokens.T).reshape(features, -1)
    gate_act, up_act = row_exchange(
        contract_rows(panel_t, gate_weight).astype(BF16),
        contract_rows(panel_t, up_weight).astype(BF16),
        hidden_grad,
    )
    share = (contract_cols(gate_weight, gate_act) + contract_cols(up_weight, up_act)).astype(BF16)
    gate_local = jnp.dot(panel_t, gate_act, preferred_element_type=F32).astype(BF16)
    up_local = jnp.dot(panel_t, up_act, preferred_element_type=F32).astype(BF16)
    gate_sum, up_sum, input_sum = sum_grads(gate_local, up_local, share)
    return (input_sum.T, gate_sum, up_sum)


def solution(mesh):
    return jax.shard_map(
        body,
        mesh=mesh,
        in_specs=(
            P("dp", ("row", "col")),
            P(("dp", "row"), "col"),
            P("row", "col"),
            P("row", "col"),
        ),
        out_specs=(P("dp", ("row", "col")), P("row", "col"), P("row", "col")),
        check_vma=False,
    )
```

time: 455 us -> 155 us (0.34)
  waiting for transfers between devices: 402 us -> 0 us
  Pallas kernels: 0 us -> 137 us
  blocking collectives: 15.9 us -> 0 us
  between operations: 13.9 us -> 0.72 us
    all_gather x2 -> x0, waiting for transfers between devices: 180 us -> none  [the longest x1 94 us: body(): lax.all_gather(gate_act, 'row', axis=0, tiled=True)]
    reduce_scatter x1 -> x0, waiting for transfers between devices: 145 us -> none  [body(): lax.psum_scatter(jnp.concatenate([jnp.dot(panel, gate_weight, preferred_e...]
    pallas_call x0 -> x3, Pallas kernels: none -> 137 us  [the longest x1 88.3 us: row_exchange(): pl.pallas_call(row_kernel, out_shape=[jax.ShapeDtypeStruct(shape, BF16)]...]
    psum x1 -> x0, waiting for transfers between devices: 50.5 us -> none  [body(): lax.psum(gate_local.astype(jnp.bfloat16), 'dp').astype(jnp.float32)]
    unnamed x6 -> x0, waiting for transfers between devices: 26.3 us -> none
    all_gather x1 -> x0, blocking collectives: 15.9 us -> none  [body(): panel = lax.all_gather(tokens, 'col', axis=1, tiled=True)]
  transfers between devices with their start and end apart: 5 -> 0, of which waited for: 5 -> 0; matrix products, arithmetic and copies ran while one was open for 3% -> 0% of each run, Pallas kernels for 0% -> 0%
where the time goes in v1:
time: 155 us; the launch traced here: 154 us
  Pallas kernels  137 us (88%)
  matrix products  11.7 us (8%)
  local copies, waits for them, and re-layouts  4.91 us (3%)
    pallas_call x1, Pallas kernels, row_exchange(): pl.pallas_call(row_kernel, out_shape=[jax.ShapeDtypeStruct(shape, BF16)]...  88.3 us
    pallas_call x1, Pallas kernels, sum_grads(): pl.pallas_call(sum_kernel, out_shape=[jax.ShapeDtypeStruct(shape, BF16)]...  36.1 us
    pallas_call x1, Pallas kernels, gather_tokens(): pl.pallas_call(gather_kernel, out_shape=jax.ShapeDtypeStruct((NC, rows, t...  12.5 us
    dot_general x2, matrix products, contract_rows(): lax.dot_general(left, right, (((0,), (0,)), ((), ())), preferred_element_...  5.02 us
    unnamed x15, local copies, waits for them, and re-layouts  4.91 us
    dot_general x2, matrix products, contract_cols(): lax.dot_general(left, right, (((1,), (1,)), ((), ())), preferred_element_...  3.62 us

profile of v1, /device:TPU:1, one launch (start us, length us, event | category | flops | bytes accessed | tf_op | source)
XLA Modules:
  0.0 154.3 jit_solution(3398395219241133593)
XLA Ops:
  0.6 0.0 copy-start
  0.6 12.5 %gather_tokens.1 = bf16[4,64,512]{2,1,0:T(8,128)(2,1)} custom-call(bf16[64,512]{1,0:T(8,128)(2,1)} %bitcast.45), custom_call_target="tpu_custom_call" | custom-call | tf_op jit(solution)/shard_map/gather_tokens/pallas_call | solution.py:59
  13.2 0.0 copy-start.1
  13.2 3.2 %convolution_convert_fusion = bf16[512,1664]{1,0:T(8,128)(2,1)} fusion(bf16[256,512]{1,0:T(8,128)(2,1)} %bitcast.32, bf16[256,1664]{1,0:T(8,128)(2,1)} %param.7), kind=kOutput, calls=%fused_computation | convolution fusion | flops 437059584 | bytes 2818048 | tf_op jit(solution)/shard_map/dot_general | solution.py:351
  16.4 0.0 copy-done
  16.4 0.0 copy-done.1
  16.4 1.9 %convolution_convert_fusion.1 = bf16[512,1664]{1,0:T(8,128)(2,1)} fusion(bf16[256,512]{1,0:T(8,128)(2,1)S(1)} %bitcast.33, bf16[256,1664]{1,0:T(8,128)(2,1)S(1)} %copy-done), kind=kOutput, calls=%fused_computation.1 | convolution fusion | flops 437059584 | bytes 2818048 | tf_op jit(solution)/shard_map/dot_general | solution.py:351
  18.2 88.3 %row_exchange.1 = (bf16[8,2,2,16,1664]{4,3,2,1,0:T(8,128)(2,1)}, bf16[8,2,2,16,1664]{4,3,2,1,0:T(8,128)(2,1)}) custom-call(bf16[8,2,2,16,1664]{4,3,2,1,0:T(8,128)(2,1)} %bitcast.31, bf16[8,2,2,16,1664]{4,3,2,1,0:T(8,128)(2,1)} %bitcast.30, bf16[16,1664]{1,0:T(8,128)(2,1)} %hidden_ref.1), custom_call_target="tpu_custom_call" | custom-call | tf_op jit(solution)/shard_map/row_exchange/pallas_call | solution.py:202
  106.5 0.0 copy-start.3
  106.5 2.2 %fusion.1 = f32[512,256]{0,1:T(8,128)S(1)} fusion(bf16[512,1664]{1,0:T(8,128)(2,1)} %bitcast.40, bf16[256,1664]{1,0:T(8,128)(2,1)S(1)} %copy-done), kind=kOutput, calls=%fused_computation.6 | convolution fusion | flops 436207616 | bytes 3080192 | tf_op jit(solution)/shard_map/dot_general | solution.py:355
  108.8 0.0 copy-done.3
  108.8 0.0 copy-start.2
  108.8 0.0 copy-start.4
  108.8 1.5 %convolution_convert_fusion.3 = bf16[1664,256]{0,1:T(8,128)(2,1)} fusion(bf16[256,512]{1,0:T(8,128)(2,1)S(1)} %bitcast.34, bf16[512,1664]{1,0:T(8,128)(2,1)S(1)} %bitcast.41), kind=kOutput, calls=%fused_computation.3 | convolution fusion | flops 436633600 | bytes 2818048 | tf_op jit(solution)/shard_map/dot_general | solution.py:367
  110.3 0.0 copy-done.2
  110.4 0.3 copy-done.4
  110.7 1.4 fusion
  112.0 1.5 %convolution_convert_fusion.2 = bf16[1664,256]{0,1:T(8,128)(2,1)} fusion(bf16[256,512]{1,0:T(8,128)(2,1)S(1)} %bitcast.35, bf16[512,1664]{1,0:T(8,128)(2,1)S(1)} %bitcast.39), kind=kOutput, calls=%fused_computation.2 | convolution fusion | flops 436633600 | bytes 2818048 | tf_op jit(solution)/shard_map/dot_general | solution.py:368
  113.6 36.1 %sum_grads.1 = (bf16[4,2,32,1664]{3,2,1,0:T(8,128)(2,1)}, bf16[4,2,32,1664]{3,2,1,0:T(8,128)(2,1)}, bf16[64,512]{1,0:T(8,128)(2,1)}) custom-call(bf16[4,2,32,1664]{3,2,1,0:T(8,128)(2,1)} %bitcast.36, bf16[4,2,32,1664]{3,2,1,0:T(8,128)(2,1)} %bitcast.37, bf16[4,64,512]{2,1,0:T(8,128)(2,1)} %bitcast.44), custom_call_target="tpu_custom_call" | custom-call | tf_op jit(solution)/shard_map/sum_grads/pallas_call | solution.py:327
  149.7 0.0 copy-start.5
  149.7 1.5 %copy.10 = bf16[512,64]{0,1:T(8,128)(2,1)} copy(bf16[512,64]{0,1:T(8,128)(2,1)} %bitcast.46) | data formatting | bytes 131072
  151.2 2.1 %copy.11 = bf16[256,1664]{1,0:T(8,128)(2,1)} copy(bf16[256,1664]{1,0:T(8,128)(2,1)} %bitcast.43) | data formatting | bytes 1703936
  153.4 0.0 copy-done.5
  153.4 0.9 copy.12
Async XLA Ops:
  0.6 15.7 %copy-start = (bf16[256,1664]{1,0:T(8,128)(2,1)S(1)}, bf16[256,1664]{1,0:T(8,128)(2,1)}, u32[]{:S(2)}) copy-start(bf16[256,1664]{1,0:T(8,128)(2,1)} %param.6) | copy-start | bytes 2555908
  13.2 3.2 %copy-start.1 = (bf16[4,64,512]{2,1,0:T(8,128)(2,1)S(1)}, bf16[4,64,512]{2,1,0:T(8,128)(2,1)}, u32[]{:S(2)}) copy-start(bf16[4,64,512]{2,1,0:T(8,128)(2,1)} %gather_tokens.1) | copy-start | bytes 786436
  106.5 2.3 %copy-start.3 = (bf16[8,2,2,16,1664]{4,3,2,1,0:T(8,128)(2,1)S(1)}, bf16[8,2,2,16,1664]{4,3,2,1,0:T(8,128)(2,1)}, u32[]{:S(2)}) copy-start(bf16[8,2,2,16,1664]{4,3,2,1,0:T(8,128)(2,1)} %get-tuple-element.8) | copy-start | bytes 5111812
  108.8 1.6 %copy-start.2 = (bf16[8,2,2,16,1664]{4,3,2,1,0:T(8,128)(2,1)S(1)}, bf16[8,2,2,16,1664]{4,3,2,1,0:T(8,128)(2,1)}, u32[]{:S(2)}) copy-start(bf16[8,2,2,16,1664]{4,3,2,1,0:T(8,128)(2,1)} %get-tuple-element.9) | copy-start | bytes 5111812
  108.8 1.9 %copy-start.4 = (bf16[256,1664]{1,0:T(8,128)(2,1)S(1)}, bf16[256,1664]{1,0:T(8,128)(2,1)}, u32[]{:S(2)}) copy-start(bf16[256,1664]{1,0:T(8,128)(2,1)} %param.7) | copy-start | bytes 2555908
  149.7 3.7 %copy-start.5 = (bf16[4,2,32,1664]{3,2,1,0:T(8,128)(2,1)S(1)}, bf16[4,2,32,1664]{3,2,1,0:T(8,128)(2,1)}, u32[]{:S(2)}) copy-start(bf16[4,2,32,1664]{3,2,1,0:T(8,128)(2,1)} %get-tuple-element.12) | copy-start | bytes 2555908

commit v2 on v0

v2 whole, which is shorter than its diff:
```python
import jax
import jax.numpy as jnp
from jax import lax
from jax.experimental import pallas as pl
from jax.experimental.pallas import tpu as pltpu
from jax.sharding import PartitionSpec as P

MESH = pl.DeviceIdType.MESH
F32 = jnp.float32
BF16 = jnp.bfloat16
NY, NX, NC = 8, 4, 4


def remote(src, dst, send, recv, target):
    copy = pltpu.make_async_remote_copy(
        src_ref=src,
        dst_ref=dst,
        send_sem=send,
        recv_sem=recv,
        device_id=target,
        device_id_type=MESH,
    )
    copy.start()
    return copy


def greet(targets):
    barrier = pltpu.get_barrier_semaphore()
    for target in targets:
        pl.semaphore_signal(barrier, inc=1, device_id=target, device_id_type=MESH)
    pl.semaphore_wait(barrier, len(targets))


def vmem():
    return pl.BlockSpec(memory_space=pltpu.VMEM)


def params(collective_id):
    return pltpu.CompilerParams(collective_id=collective_id, has_side_effects=True)


def gather_kernel(mine_ref, all_ref, local_sem, send_sem, recv_sem):
    col = lax.axis_index("col")
    peers = [{"col": lax.rem(col + o, NC)} for o in range(1, NC)]
    greet(peers)
    copies = [
        remote(mine_ref, all_ref.at[col], send_sem.at[o], recv_sem.at[o], peers[o])
        for o in range(NC - 1)
    ]
    own = pltpu.make_async_copy(mine_ref, all_ref.at[col], local_sem)
    own.start()
    own.wait()
    for copy in copies:
        copy.wait()


def gather_tokens(block):
    rows, tokens = block.shape
    return pl.pallas_call(
        gather_kernel,
        out_shape=jax.ShapeDtypeStruct((NC, rows, tokens), BF16),
        in_specs=[vmem()],
        out_specs=vmem(),
        scratch_shapes=[
            pltpu.SemaphoreType.DMA,
            pltpu.SemaphoreType.DMA((NC - 1,)),
            pltpu.SemaphoreType.DMA((NC - 1,)),
        ],
        compiler_params=params(0),
        name="gather_tokens",
    )(block)


def main_kernel(
    gate_ref, up_ref, hidden_ref, panel_ref, gate_weight_ref, up_weight_ref,
    gate_out, up_out, input_out,
    core_in, ring_out, ring_in, own, pair_out, pair_in, acts,
    local, dp_out, dp_in, share_out, share_in, share_own,
    core_send, core_recv, ring_send, ring_recv, pair_send, pair_recv,
    swap_send, swap_recv, turn_send, turn_recv, fwd_send, fwd_recv,
    dp_send, dp_recv, back_send, back_recv, share_send, share_recv,
):
    row = lax.axis_index("row")
    dp = lax.axis_index("dp")
    col = lax.axis_index("col")
    y = lax.div(row, 4)
    core = lax.rem(row, 2)
    zh = lax.rem(lax.div(row, 2), 2)
    low = lax.rem(row, 4)
    y_next = (
        {"row": lax.rem(y + 1, NY) * 4 + low},
        {"row": lax.rem(y + NY - 1, NY) * 4 + low},
    )
    x_next = ({"dp": lax.rem(dp + 1, NX)}, {"dp": lax.rem(dp + NX - 1, NX)})
    partner = {"row": y * 4 + zh * 2 + (1 - core)}
    pair = {"row": y * 4 + (1 - zh) * 2 + core}
    peers = [{"col": lax.rem(col + o, NC)} for o in range(1, NC)]
    greet([*y_next, partner, pair, *x_next, *peers])

    ins = (gate_ref, up_ref)
    outs = (gate_out, up_out)
    zhs = (1 - zh, zh)
    BOTH = ((0, 0), (0, 1), (1, 0), (1, 1))
    sent = []

    def send(*args):
        copy = remote(*args)
        sent.append(copy)
        return copy

    def hops(w, d):
        return NY // 2 if w == d else NY // 2 - 1

    def at_y(d, ahead):
        return lax.rem(y + NY + (ahead if d == 0 else -ahead), NY)

    MOST = NY // 2
    core_copies = {}
    for s in range(MOST):
        for w, d in BOTH:
            if s < hops(w, d):
                core_copies[w, d, s] = send(
                    ins[w].at[at_y(d, hops(w, d) - s), :, 1 - core],
                    core_in.at[w, d * MOST + s],
                    core_send.at[w, d * MOST + s],
                    core_recv.at[w, d * MOST + s],
                    partner,
                )
    for w in range(2):
        free = (1 - w) * MOST + MOST - 1
        core_copies[w] = send(
            ins[w].at[y, :, 1 - core],
            core_in.at[w, free],
            core_send.at[w, free],
            core_recv.at[w, free],
            partner,
        )
    ring = {}
    for s in range(MOST):
        for w, d in BOTH:
            if s >= hops(w, d):
                continue
            core_copies[w, d, s].wait_recv()
            for j in range(2):
                total = (
                    ins[w][at_y(d, hops(w, d) - s), zhs[j], core].astype(F32)
                    + core_in[w, d * MOST + s, zhs[j]].astype(F32)
                )
                if s > 0:
                    ring[w, d, j, s - 1].wait_recv()
                    total = total + ring_in[w, d, j, s - 1].astype(F32)
                ring_out[w, d, j, s] = total.astype(BF16)
                ring[w, d, j, s] = send(
                    ring_out.at[w, d, j, s],
                    ring_in.at[w, d, j, s],
                    ring_send.at[w, d, j, s],
                    ring_recv.at[w, d, j, s],
                    y_next[d],
                )
    for w in range(2):
        core_copies[w].wait_recv()
    pairs = []
    for j in range(2):
        for w in range(2):
            total = (
                ins[w][y, zhs[j], core].astype(F32)
                + core_in[w, (1 - w) * MOST + MOST - 1, zhs[j]].astype(F32)
            )
            for d in (1 - w, w):
                last = hops(w, d) - 1
                ring[w, d, j, last].wait_recv()
                total = total + ring_in[w, d, j, last].astype(F32)
            if j == 0:
                pair_out[w] = total.astype(BF16)
                pairs.append(
                    send(pair_out.at[w], pair_in.at[w], pair_send.at[w], pair_recv.at[w], pair)
                )
            else:
                own[w] = total
    for copy in pairs:
        copy.wait_recv()
    gate = own[0] + pair_in[0].astype(F32)
    up = own[1] + pair_in[1].astype(F32)
    sigma = jax.nn.sigmoid(gate)
    upstream = hidden_ref[...].astype(F32)
    acts[0, y, zh, core] = (upstream * up * sigma * (1.0 + gate * (1.0 - sigma))).astype(BF16)
    acts[1, y, zh, core] = (upstream * gate * sigma).astype(BF16)

    steps = []

    def plan(time, step, *args):
        steps.append((time, len(steps), step, args))

    turn = {}
    fwd = {}
    swap = [
        send(
            acts.at[w, y, zh, core], acts.at[w, y, zh, core], swap_send.at[w], swap_recv.at[w], pair
        )
        for w in range(2)
    ]

    def pass_on(w, d, j, s):
        here = acts.at[w, at_y(d, -s), zhs[j], core]
        if s > 0:
            turn[w, d, j, s - 1].wait_recv()
        if s < hops(w, d):
            turn[w, d, j, s] = send(
                here, here, turn_send.at[w, d, j, s], turn_recv.at[w, d, j, s], y_next[d]
            )
        if s > 0 or d == 0:
            fwd[w, d, j, s] = send(
                here, here, fwd_send.at[w, d, j, s], fwd_recv.at[w, d, j, s], partner
            )

    def arrive(w):
        swap[w].wait_recv()
        for d in range(2):
            pass_on(w, d, 0, 0)

    for w in range(2):
        for d in range(2):
            pass_on(w, d, 1, 0)
            for s in range(1, hops(w, d) + 1):
                plan(2.3 * s + 0.5 * w, pass_on, w, d, 1, s)
                plan((9.0, 13.0)[w] + 2.3 * s, pass_on, w, d, 0, s)
        plan((9.0, 13.0)[w], arrive, w)

    order = [lax.rem(dp + o, NX) for o in (NX - 1, 1, 2, 0)]
    slots = ((0, 2, 1, 3), (1, 2, 0, 3))
    half = local.shape[3]
    width = local.shape[4]
    dps = {}
    back = {}

    def gathered(w):
        for key, copy in fwd.items():
            if key[0] == w:
                copy.wait_recv()

    def dp_send_on(w, d, s, src):
        dps[w, d, s] = send(
            src, dp_in.at[w, d, s], dp_send.at[w, d, s], dp_recv.at[w, d, s], x_next[d]
        )

    def product(w, k):
        value = jnp.dot(
            panel_ref[order[k]],
            acts[w].reshape(-1, width),
            preferred_element_type=F32,
        ).astype(BF16)
        for d in range(2):
            local[w, k, d] = value[d * half : (d + 1) * half]
        if k < 2:
            dp_send_on(w, k, 0, local.at[w, k, k])

    def dp_step(w, d, s):
        dps[w, d, s - 1].wait_recv()
        total = local[w, slots[d][s], d].astype(F32) + dp_in[w, d, s - 1].astype(F32)
        if s < NX - 1:
            dp_out[w, d, s - 1] = total.astype(BF16)
            dp_send_on(w, d, s, dp_out.at[w, d, s - 1])
        else:
            outs[w][dp, d] = total.astype(BF16)
            back_on(w, d, 0)

    def back_on(w, d, s):
        if s > 0:
            back[w, d, s - 1].wait_recv()
        if s < NX - 1:
            at = lax.rem(dp + NX + (-s if d == 0 else s), NX)
            back[w, d, s] = send(
                outs[w].at[at, d],
                outs[w].at[at, d],
                back_send.at[w, d, s],
                back_recv.at[w, d, s],
                x_next[d],
            )

    starts = (20.0, 24.5)
    for w in range(2):
        plan(starts[w], gathered, w)
        for k in range(NX):
            plan(starts[w] + 0.1 + k, product, w, k)
        for d in range(2):
            for s in range(1, NX):
                plan(starts[w] + 1.5 + 4.8 * s, dp_step, w, d, s)
                plan(starts[w] + 1.5 + 4.8 * (NX - 1 + s), back_on, w, d, s)

    share = {}

    def share_step(o):
        block = lax.rem(col + o + 1, NC)
        total = lax.dot_general(
            gate_weight_ref[block], acts[0].reshape(-1, width), (((1,), (1,)), ((), ())),
            preferred_element_type=F32,
        ) + lax.dot_general(
            up_weight_ref[block], acts[1].reshape(-1, width), (((1,), (1,)), ((), ())),
            preferred_element_type=F32,
        )
        if o < NC - 1:
            share_out[o] = total.astype(BF16)
            share[o] = send(
                share_out.at[o], share_in.at[o], share_send.at[o], share_recv.at[o], peers[o]
            )
        else:
            share_own[...] = total

    def share_end():
        total = share_own[...]
        for o in range(NC - 1):
            share[o].wait_recv()
            total = total + share_in[o].astype(F32)
        input_out[...] = total.astype(BF16)

    for o in range(NC):
        plan(starts[1] + 5.0 + 2.4 * o, share_step, o)
    plan(starts[1] + 22.0, share_end)

    for _, _, step, args in sorted(steps, key=lambda item: item[:2]):
        step(*args)
    for copy in sent:
        copy.wait_send()


def main_call(gate, up, hidden, panel, gate_weight, up_weight):
    rows, width = hidden.shape
    features = gate_weight.shape[0]
    tokens = gate.shape[0]
    part = features // NC
    half = features // NX // 2
    shape = (NY, 2, 2, rows, width)
    most = NY // 2
    dma = pltpu.SemaphoreType.DMA
    vm = pltpu.VMEM
    gate_sum, up_sum, input_sum = pl.pallas_call(
        main_kernel,
        out_shape=[jax.ShapeDtypeStruct((NX, 2, half, width), BF16)] * 2
        + [jax.ShapeDtypeStruct((part, tokens), BF16)],
        in_specs=[vmem()] * 6,
        out_specs=[vmem()] * 3,
        scratch_shapes=[
            vm((2, 2 * most, 2, rows, width), BF16),
            vm((2, 2, 2, most, rows, width), BF16),
            vm((2, 2, 2, most, rows, width), BF16),
            vm((2, rows, width), F32),
            vm((2, rows, width), BF16),
            vm((2, rows, width), BF16),
            vm((2, *shape), BF16),
            vm((2, NX, 2, half, width), BF16),
            vm((2, 2, NX - 2, half, width), BF16),
            vm((2, 2, NX - 1, half, width), BF16),
            vm((NC - 1, part, tokens), BF16),
            vm((NC - 1, part, tokens), BF16),
            vm((part, tokens), F32),
            *[dma((2, 2 * most))] * 2,
            *[dma((2, 2, 2, most))] * 2,
            *[dma((2,))] * 2,
            *[dma((2,))] * 2,
            *[dma((2, 2, 2, most))] * 2,
            *[dma((2, 2, 2, most + 1))] * 2,
            *[dma((2, 2, NX - 1))] * 2,
            *[dma((2, 2, NX - 1))] * 2,
            *[dma((NC - 1,))] * 2,
        ],
        compiler_params=params(1),
        name="main",
    )(
        gate.reshape(shape),
        up.reshape(shape),
        hidden,
        panel.reshape(NX, features // NX, tokens),
        gate_weight.reshape(NC, part, width),
        up_weight.reshape(NC, part, width),
    )
    return input_sum.T, gate_sum.reshape(features, width), up_sum.reshape(features, width)


def contract_rows(left, right):
    return lax.dot_general(left, right, (((0,), (0,)), ((), ())), preferred_element_type=F32)


def body(tokens, hidden_grad, gate_weight, up_weight):
    features = gate_weight.shape[0]
    panel_t = gather_tokens(tokens.T).reshape(features, -1)
    return main_call(
        contract_rows(panel_t, gate_weight).astype(BF16),
        contract_rows(panel_t, up_weight).astype(BF16),
        hidden_grad,
        panel_t,
        gate_weight,
        up_weight,
    )


def solution(mesh):
    return jax.shard_map(
        body,
        mesh=mesh,
        in_specs=(
            P("dp", ("row", "col")),
            P(("dp", "row"), "col"),
            P("row", "col"),
            P("row", "col"),
        ),
        out_specs=(P("dp", ("row", "col")), P("row", "col"), P("row", "col")),
        check_vma=False,
    )
```

time: 455 us -> 128 us (0.28)
  waiting for transfers between devices: 402 us -> 0 us
  Pallas kernels: 0 us -> 117 us
  blocking collectives: 15.9 us -> 0 us
  between operations: 13.9 us -> 0.67 us
  matrix products: 12.2 us -> 5 us
    all_gather x2 -> x0, waiting for transfers between devices: 180 us -> none  [the longest x1 94 us: body(): lax.all_gather(gate_act, 'row', axis=0, tiled=True)]
    reduce_scatter x1 -> x0, waiting for transfers between devices: 145 us -> none  [body(): lax.psum_scatter(jnp.concatenate([jnp.dot(panel, gate_weight, preferred_e...]
    pallas_call x0 -> x2, Pallas kernels: none -> 117 us  [the longest x1 104 us: main_call(): pl.pallas_call(main_kernel, out_shape=[jax.ShapeDtypeStruct((NX, 2, half,...]
    psum x1 -> x0, waiting for transfers between devices: 50.5 us -> none  [body(): lax.psum(gate_local.astype(jnp.bfloat16), 'dp').astype(jnp.float32)]
    unnamed x6 -> x0, waiting for transfers between devices: 26.3 us -> none
    all_gather x1 -> x0, blocking collectives: 15.9 us -> none  [body(): panel = lax.all_gather(tokens, 'col', axis=1, tiled=True)]
    dot_general x4 -> x0, matrix products: 6.17 us -> none  [the longest x2 3.67 us: contract_cols(): lax.dot_general(left, right, (((1,), (1,)), ((), ())), preferred_element_...]
  transfers between devices with their start and end apart: 5 -> 0, of which waited for: 5 -> 0; matrix products, arithmetic and copies ran while one was open for 3% -> 0% of each run, Pallas kernels for 0% -> 0%
where the time goes in v2:
time: 128 us; the launch traced here: 127 us
  Pallas kernels  117 us (91%)
  matrix products  5 us (4%)
  local copies, waits for them, and re-layouts  4.58 us (4%)
    pallas_call x1, Pallas kernels, main_call(): pl.pallas_call(main_kernel, out_shape=[jax.ShapeDtypeStruct((NX, 2, half,...  104 us
    pallas_call x1, Pallas kernels, gather_tokens(): pl.pallas_call(gather_kernel, out_shape=jax.ShapeDtypeStruct((NC, rows, t...  12.5 us
    dot_general x2, matrix products, contract_rows(): lax.dot_general(left, right, (((0,), (0,)), ((), ())), preferred_element_...  5 us
    unnamed x9, local copies, waits for them, and re-layouts  4.58 us

profile of v2, /device:TPU:1, one launch (start us, length us, event | category | flops | bytes accessed | tf_op | source)
XLA Modules:
  0.0 127.2 jit_solution(8704754452643407136)
XLA Ops:
  0.6 0.0 copy-start.1
  0.6 12.5 %gather_tokens.1.panel_ref = bf16[4,64,512]{2,1,0:T(8,128)(2,1)} custom-call(bf16[64,512]{1,0:T(8,128)(2,1)} %bitcast.21), custom_call_target="tpu_custom_call" | custom-call | tf_op jit(solution)/shard_map/gather_tokens/pallas_call | solution.py:59
  13.2 0.0 copy-start
  13.2 3.1 %convolution_convert_fusion = bf16[512,1664]{1,0:T(8,128)(2,1)} fusion(bf16[256,512]{1,0:T(8,128)(2,1)} %bitcast.15, bf16[256,1664]{1,0:T(8,128)(2,1)} %param.7), kind=kOutput, calls=%fused_computation | convolution fusion | flops 437059584 | bytes 2818048 | tf_op jit(solution)/shard_map/dot_general | solution.py:380
  16.3 0.0 copy-done.1
  16.3 0.0 copy-done
  16.3 1.9 %convolution_convert_fusion.1 = bf16[512,1664]{1,0:T(8,128)(2,1)} fusion(bf16[256,512]{1,0:T(8,128)(2,1)S(1)} %bitcast.16, bf16[256,1664]{1,0:T(8,128)(2,1)S(1)} %copy-done.1), kind=kOutput, calls=%fused_computation.1 | convolution fusion | flops 437059584 | bytes 2818048 | tf_op jit(solution)/shard_map/dot_general | solution.py:380
  18.2 104.4 %main.1 = (bf16[4,2,32,1664]{3,2,1,0:T(8,128)(2,1)}, bf16[4,2,32,1664]{3,2,1,0:T(8,128)(2,1)}, bf16[64,512]{1,0:T(8,128)(2,1)}) custom-call(bf16[8,2,2,16,1664]{4,3,2,1,0:T(8,128)(2,1)} %bitcast.14, bf16[8,2,2,16,1664]{4,3,2,1,0:T(8,128)(2,1)} %bitcast.13, bf16[16,1664]{1,0:T(8,128)(2,1)} %hidden_ref.1, bf16[4,64,512]{2,1,0:T(8,128)(2,1)} %gather_tokens.1.panel_ref, ...), custom_call_target="tpu_custom_call" | custom-call | tf_op jit(solution)/shard_map/main/pallas_call | solution.py:336
  122.6 0.0 copy-start.2
  122.7 1.5 %copy.10 = bf16[512,64]{0,1:T(8,128)(2,1)} copy(bf16[512,64]{0,1:T(8,128)(2,1)} %bitcast.22) | data formatting | bytes 131072
  124.2 2.1 %copy.11 = bf16[256,1664]{1,0:T(8,128)(2,1)} copy(bf16[256,1664]{1,0:T(8,128)(2,1)} %bitcast.20) | data formatting | bytes 1703936
  126.3 0.0 copy-done.2
  126.3 0.9 copy.12
Async XLA Ops:
  0.6 15.7 %copy-start.1 = (bf16[256,1664]{1,0:T(8,128)(2,1)S(1)}, bf16[256,1664]{1,0:T(8,128)(2,1)}, u32[]{:S(2)}) copy-start(bf16[256,1664]{1,0:T(8,128)(2,1)} %param.6) | copy-start | bytes 2555908
  13.2 3.1 %copy-start = (bf16[4,64,512]{2,1,0:T(8,128)(2,1)S(1)}, bf16[4,64,512]{2,1,0:T(8,128)(2,1)}, u32[]{:S(2)}) copy-start(bf16[4,64,512]{2,1,0:T(8,128)(2,1)} %gather_tokens.1.panel_ref) | copy-start | bytes 786436
  122.6 3.7 %copy-start.2 = (bf16[4,2,32,1664]{3,2,1,0:T(8,128)(2,1)S(1)}, bf16[4,2,32,1664]{3,2,1,0:T(8,128)(2,1)}, u32[]{:S(2)}) copy-start(bf16[4,2,32,1664]{3,2,1,0:T(8,128)(2,1)} %get-tuple-element.8) | copy-start | bytes 2555908

commit v3 on v2

--- a/solution.py
+++ b/solution.py
@@ -39,43 +39,13 @@
     return pltpu.CompilerParams(collective_id=collective_id, has_side_effects=True)
 
 
-def gather_kernel(mine_ref, all_ref, local_sem, send_sem, recv_sem):
-    col = lax.axis_index("col")
-    peers = [{"col": lax.rem(col + o, NC)} for o in range(1, NC)]
-    greet(peers)
-    copies = [
-        remote(mine_ref, all_ref.at[col], send_sem.at[o], recv_sem.at[o], peers[o])
-        for o in range(NC - 1)
-    ]
-    own = pltpu.make_async_copy(mine_ref, all_ref.at[col], local_sem)
-    own.start()
-    own.wait()
-    for copy in copies:
-        copy.wait()
-
-
-def gather_tokens(block):
-    rows, tokens = block.shape
-    return pl.pallas_call(
-        gather_kernel,
-        out_shape=jax.ShapeDtypeStruct((NC, rows, tokens), BF16),
-        in_specs=[vmem()],
-        out_specs=vmem(),
-        scratch_shapes=[
-            pltpu.SemaphoreType.DMA,
-            pltpu.SemaphoreType.DMA((NC - 1,)),
-            pltpu.SemaphoreType.DMA((NC - 1,)),
-        ],
-        compiler_params=params(0),
-        name="gather_tokens",
-    )(block)
-
-
 def main_kernel(
-    gate_ref, up_ref, hidden_ref, panel_ref, gate_weight_ref, up_weight_ref,
+    tokens_ref, hidden_ref, gate_weight_ref, up_weight_ref,
     gate_out, up_out, input_out,
+    panel_ref, panel_rows, parts, relay_in,
     core_in, ring_out, ring_in, own, pair_out, pair_in, acts,
     local, dp_out, dp_in, share_out, share_in, share_own,
+    own_sem, panel_send, panel_recv, relay_send, relay_recv,
     core_send, core_recv, ring_send, ring_recv, pair_send, pair_recv,
     swap_send, swap_recv, turn_send, turn_recv, fwd_send, fwd_recv,
     dp_send, dp_recv, back_send, back_recv, share_send, share_recv,
@@ -93,11 +63,19 @@
     )
     x_next = ({"dp": lax.rem(dp + 1, NX)}, {"dp": lax.rem(dp + NX - 1, NX)})
     partner = {"row": y * 4 + zh * 2 + (1 - core)}
-    pair = {"row": y * 4 + (1 - zh) * 2 + core}
+    z = zh * NC + col
+
+    def at_z(hops):
+        there = lax.rem(z + 2 * NC + hops, 2 * NC)
+        return {"row": y * 4 + lax.div(there, NC) * 2 + core, "col": lax.rem(there, NC)}
+
+    z_near = (at_z(-1), at_z(1))
+    z_far = (at_z(-3), at_z(3))
+    z_from = (lax.div(lax.rem(z + 1, 2 * NC), NC), lax.div(lax.rem(z + 2 * NC - 1, 2 * NC), NC))
     peers = [{"col": lax.rem(col + o, NC)} for o in range(1, NC)]
-    greet([*y_next, partner, pair, *x_next, *peers])
-
-    ins = (gate_ref, up_ref)
+    greet([*y_next, partner, *z_near, *z_far, *x_next, *peers])
+
+    weights = (gate_weight_ref, up_weight_ref)
     outs = (gate_out, up_out)
     zhs = (1 - zh, zh)
     BOTH = ((0, 0), (0, 1), (1, 0), (1, 1))
@@ -114,71 +92,124 @@
     def at_y(d, ahead):
         return lax.rem(y + NY + (ahead if d == 0 else -ahead), NY)
 
+    half = local.shape[3]
+    width = local.shape[4]
+    rows = hidden_ref.shape[0]
+    panels = [
+        send(tokens_ref, panel_ref.at[col], panel_send.at[o], panel_recv.at[o], peers[o])
+        for o in range(NC - 1)
+    ]
+    mine = pltpu.make_async_copy(tokens_ref, panel_ref.at[col], own_sem)
+    mine.start()
+    mine.wait()
+    for copy in panels:
+        copy.wait_recv()
+    panel_rows[...] = (
+        panel_ref[...].reshape(-1, panel_ref.shape[2]).T.reshape(panel_rows.shape)
+    )
+
+    steps = []
+
+    def plan(time, step, *args):
+        steps.append((time, len(steps), step, args))
+
+    def run():
+        for _, _, step, args in sorted(steps, key=lambda item: item[:2]):
+            step(*args)
+        steps.clear()
+
     MOST = NY // 2
     core_copies = {}
-    for s in range(MOST):
-        for w, d in BOTH:
-            if s < hops(w, d):
-                core_copies[w, d, s] = send(
-                    ins[w].at[at_y(d, hops(w, d) - s), :, 1 - core],
-                    core_in.at[w, d * MOST + s],
-                    core_send.at[w, d * MOST + s],
-                    core_recv.at[w, d * MOST + s],
-                    partner,
-                )
+
+    def slot_of(w, d, s):
+        return d * MOST + s if d is not None else (1 - w) * MOST + MOST - 1
+
+    def block_of(w, d, s):
+        return at_y(d, hops(w, d) - s) if d is not None else y
+
+    def multiply(w, d, s):
+        block, slot = block_of(w, d, s), slot_of(w, d, s)
+        parts[w, slot] = (
+            jnp.dot(
+                panel_rows[block],
+                weights[w][...].reshape(-1, width),
+                preferred_element_type=F32,
+            )
+            .astype(BF16)
+            .reshape(2, 2, rows, width)
+        )
+        core_copies[w, d, s] = send(
+            parts.at[w, slot, :, 1 - core],
+            core_in.at[w, slot],
+            core_send.at[w, slot],
+            core_recv.at[w, slot],
+            partner,
+        )
+
+    ring = {}
+    seen = set()
+
+    def here(w, d, s, j):
+        if (w, d, s) not in seen:
+            seen.add((w, d, s))
+            core_copies[w, d, s].wait_recv()
+        slot = slot_of(w, d, s)
+        return parts[w, slot, zhs[j], core].astype(F32) + core_in[w, slot, zhs[j]].astype(F32)
+
+    def ring_step(w, d, s, j):
+        total = here(w, d, s, j)
+        if s > 0:
+            ring[w, d, j, s - 1].wait_recv()
+            total = total + ring_in[w, d, j, s - 1].astype(F32)
+        ring_out[w, d, j, s] = total.astype(BF16)
+        ring[w, d, j, s] = send(
+            ring_out.at[w, d, j, s],
+            ring_in.at[w, d, j, s],
+            ring_send.at[w, d, j, s],
+            ring_recv.at[w, d, j, s],
+            y_next[d],
+        )
+
+    near = {}
+    far = {}
+
+    def ring_end(w, j):
+        total = here(w, None, 0, j)
+        for d in (1 - w, w):
+            last = hops(w, d) - 1
+            ring[w, d, j, last].wait_recv()
+            total = total + ring_in[w, d, j, last].astype(F32)
+        if j == 0:
+            pair_out[w] = total.astype(BF16)
+            near[w, 0] = send(
+                pair_out.at[w],
+                relay_in.at[w, 0],
+                relay_send.at[w, 0],
+                relay_recv.at[w, 0],
+                z_near[w],
+            )
+        else:
+            own[w] = total
+
+    def relay(w):
+        near[w, 0].wait_recv()
+        far[w, 0] = send(
+            relay_in.at[w, 0], pair_in.at[w], pair_send.at[w], pair_recv.at[w], z_far[w]
+        )
+
+    for w, d in BOTH:
+        for s in range(hops(w, d)):
+            plan(3.5 * (s - 1) - 1.0, multiply, w, d, s)
+            for j in range(2):
+                plan(3.5 * s + 6.0 * j, ring_step, w, d, s, j)
     for w in range(2):
-        free = (1 - w) * MOST + MOST - 1
-        core_copies[w] = send(
-            ins[w].at[y, :, 1 - core],
-            core_in.at[w, free],
-            core_send.at[w, free],
-            core_recv.at[w, free],
-            partner,
-        )
-    ring = {}
-    for s in range(MOST):
-        for w, d in BOTH:
-            if s >= hops(w, d):
-                continue
-            core_copies[w, d, s].wait_recv()
-            for j in range(2):
-                total = (
-                    ins[w][at_y(d, hops(w, d) - s), zhs[j], core].astype(F32)
-                    + core_in[w, d * MOST + s, zhs[j]].astype(F32)
-                )
-                if s > 0:
-                    ring[w, d, j, s - 1].wait_recv()
-                    total = total + ring_in[w, d, j, s - 1].astype(F32)
-                ring_out[w, d, j, s] = total.astype(BF16)
-                ring[w, d, j, s] = send(
-                    ring_out.at[w, d, j, s],
-                    ring_in.at[w, d, j, s],
-                    ring_send.at[w, d, j, s],
-                    ring_recv.at[w, d, j, s],
-                    y_next[d],
-                )
+        plan(9.0, multiply, w, None, 0)
+        plan(14.0, ring_end, w, 0)
+        plan(17.0, relay, w)
+        plan(20.0, ring_end, w, 1)
+    run()
     for w in range(2):
-        core_copies[w].wait_recv()
-    pairs = []
-    for j in range(2):
-        for w in range(2):
-            total = (
-                ins[w][y, zhs[j], core].astype(F32)
-                + core_in[w, (1 - w) * MOST + MOST - 1, zhs[j]].astype(F32)
-            )
-            for d in (1 - w, w):
-                last = hops(w, d) - 1
-                ring[w, d, j, last].wait_recv()
-                total = total + ring_in[w, d, j, last].astype(F32)
-            if j == 0:
-                pair_out[w] = total.astype(BF16)
-                pairs.append(
-                    send(pair_out.at[w], pair_in.at[w], pair_send.at[w], pair_recv.at[w], pair)
-                )
-            else:
-                own[w] = total
-    for copy in pairs:
-        copy.wait_recv()
+        far[w, 0].wait_recv()
     gate = own[0] + pair_in[0].astype(F32)
     up = own[1] + pair_in[1].astype(F32)
     sigma = jax.nn.sigmoid(gate)
@@ -186,19 +217,26 @@
     acts[0, y, zh, core] = (upstream * up * sigma * (1.0 + gate * (1.0 - sigma))).astype(BF16)
     acts[1, y, zh, core] = (upstream * gate * sigma).astype(BF16)
 
-    steps = []
-
-    def plan(time, step, *args):
-        steps.append((time, len(steps), step, args))
-
     turn = {}
     fwd = {}
-    swap = [
-        send(
-            acts.at[w, y, zh, core], acts.at[w, y, zh, core], swap_send.at[w], swap_recv.at[w], pair
-        )
-        for w in range(2)
-    ]
+    for w in range(2):
+        near[w, 1] = send(
+            acts.at[w, y, zh, core],
+            relay_in.at[w, 1],
+            relay_send.at[w, 1],
+            relay_recv.at[w, 1],
+            z_near[w],
+        )
+
+    def relay_act(w):
+        near[w, 1].wait_recv()
+        far[w, 1] = send(
+            relay_in.at[w, 1],
+            acts.at[w, y, z_from[w], core],
+            swap_send.at[w],
+            swap_recv.at[w],
+            z_far[w],
+        )
 
     def pass_on(w, d, j, s):
         here = acts.at[w, at_y(d, -s), zhs[j], core]
@@ -214,7 +252,7 @@
             )
 
     def arrive(w):
-        swap[w].wait_recv()
+        far[w, 1].wait_recv()
         for d in range(2):
             pass_on(w, d, 0, 0)
 
@@ -223,13 +261,12 @@
             pass_on(w, d, 1, 0)
             for s in range(1, hops(w, d) + 1):
                 plan(2.3 * s + 0.5 * w, pass_on, w, d, 1, s)
-                plan((9.0, 13.0)[w] + 2.3 * s, pass_on, w, d, 0, s)
-        plan((9.0, 13.0)[w], arrive, w)
+                plan((8.0, 9.0)[w] + 2.3 * s, pass_on, w, d, 0, s)
+        plan(2.2, relay_act, w)
+        plan((8.0, 9.0)[w], arrive, w)
 
     order = [lax.rem(dp + o, NX) for o in (NX - 1, 1, 2, 0)]
     slots = ((0, 2, 1, 3), (1, 2, 0, 3))
-    half = local.shape[3]
-    width = local.shape[4]
     dps = {}
     back = {}
 
@@ -277,7 +314,7 @@
                 x_next[d],
             )
 
-    starts = (20.0, 24.5)
+    starts = (18.5, 22.0)
     for w in range(2):
         plan(starts[w], gathered, w)
         for k in range(NX):
@@ -317,16 +354,15 @@
         plan(starts[1] + 5.0 + 2.4 * o, share_step, o)
     plan(starts[1] + 22.0, share_end)
 
-    for _, _, step, args in sorted(steps, key=lambda item: item[:2]):
-        step(*args)
+    run()
     for copy in sent:
         copy.wait_send()
 
 
-def main_call(gate, up, hidden, panel, gate_weight, up_weight):
+def main_call(tokens_t, hidden, gate_weight, up_weight):
     rows, width = hidden.shape
     features = gate_weight.shape[0]
-    tokens = gate.shape[0]
+    tokens = tokens_t.shape[1]
     part = features // NC
     half = features // NX // 2
     shape = (NY, 2, 2, rows, width)
@@ -337,9 +373,13 @@
         main_kernel,
         out_shape=[jax.ShapeDtypeStruct((NX, 2, half, width), BF16)] * 2
         + [jax.ShapeDtypeStruct((part, tokens), BF16)],
-        in_specs=[vmem()] * 6,
+        in_specs=[vmem()] * 4,
         out_specs=[vmem()] * 3,
         scratch_shapes=[
+            vm((NC, part, tokens), BF16),
+            vm((NY, tokens // NY, features), BF16),
+            vm((2, 2 * most, 2, 2, rows, width), BF16),
+            vm((2, 2, rows, width), BF16),
             vm((2, 2 * most, 2, rows, width), BF16),
             vm((2, 2, 2, most, rows, width), BF16),
             vm((2, 2, 2, most, rows, width), BF16),
@@ -353,6 +393,9 @@
             vm((NC - 1, part, tokens), BF16),
             vm((NC - 1, part, tokens), BF16),
             vm((part, tokens), F32),
+            dma,
+            *[dma((NC - 1,))] * 2,
+            *[dma((2, 2))] * 2,
             *[dma((2, 2 * most))] * 2,
             *[dma((2, 2, 2, most))] * 2,
             *[dma((2,))] * 2,
@@ -366,31 +409,16 @@
         compiler_params=params(1),
         name="main",
     )(
-        gate.reshape(shape),
-        up.reshape(shape),
+        tokens_t,
         hidden,
-        panel.reshape(NX, features // NX, tokens),
         gate_weight.reshape(NC, part, width),
         up_weight.reshape(NC, part, width),
     )
     return input_sum.T, gate_sum.reshape(features, width), up_sum.reshape(features, width)
 
 
-def contract_rows(left, right):
-    return lax.dot_general(left, right, (((0,), (0,)), ((), ())), preferred_element_type=F32)
-
-
 def body(tokens, hidden_grad, gate_weight, up_weight):
-    features = gate_weight.shape[0]
-    panel_t = gather_tokens(tokens.T).reshape(features, -1)
-    return main_call(
-        contract_rows(panel_t, gate_weight).astype(BF16),
-        contract_rows(panel_t, up_weight).astype(BF16),
-        hidden_grad,
-        panel_t,
-        gate_weight,
-        up_weight,
-    )
+    return main_call(tokens.T, hidden_grad, gate_weight, up_weight)
 
 
 def solution(mesh):

time: 128 us -> 119 us (0.930)
  matrix products: 5 us -> 0 us
  Pallas kernels: 117 us -> 113 us
    pallas_call x1 -> x0, Pallas kernels: 12.5 us -> none  [gather_tokens(): pl.pallas_call(gather_kernel, out_shape=jax.ShapeDtypeStruct((NC, rows, t...]
    pallas_call x1, Pallas kernels: 104 us -> 113 us  [main_call(): pl.pallas_call(main_kernel, out_shape=[jax.ShapeDtypeStruct((NX, 2, half,...]
    dot_general x2 -> x0, matrix products: 5 us -> none  [contract_rows(): lax.dot_general(left, right, (((0,), (0,)), ((), ())), preferred_element_...]
    unnamed x9 -> x5, local copies, waits for them, and re-layouts: 4.58 us -> 4.57 us
where the time goes in v3:
time: 119 us; the launch traced here: 118 us
  Pallas kernels  113 us (95%)
  local copies, waits for them, and re-layouts  4.57 us (4%)
    pallas_call x1, Pallas kernels, main_call(): pl.pallas_call(main_kernel, out_shape=[jax.ShapeDtypeStruct((NX, 2, half,...  113 us
    unnamed x5, local copies, waits for them, and re-layouts  4.57 us

profile of v3, /device:TPU:1, one launch (start us, length us, event | category | flops | bytes accessed | tf_op | source)
XLA Modules:
  0.0 117.8 jit_solution(13962627788842440496)
XLA Ops:
  0.6 112.6 %main.1 = (bf16[4,2,32,1664]{3,2,1,0:T(8,128)(2,1)}, bf16[4,2,32,1664]{3,2,1,0:T(8,128)(2,1)}, bf16[64,512]{1,0:T(8,128)(2,1)}) custom-call(bf16[64,512]{1,0:T(8,128)(2,1)} %bitcast.10, bf16[16,1664]{1,0:T(8,128)(2,1)} %hidden_ref.1, bf16[4,64,1664]{2,1,0:T(8,128)(2,1)} %bitcast.6, bf16[4,64,1664]{2,1,0:T(8,128)(2,1)} %bitcast.7), custom_call_target="tpu_custom_call" | custom-call | tf_op jit(solution)/shard_map/main/pallas_call | solution.py:372
  113.2 1.5 %copy.10 = bf16[512,64]{0,1:T(8,128)(2,1)} copy(bf16[512,64]{0,1:T(8,128)(2,1)} %bitcast.11) | data formatting | bytes 131072
  114.7 0.0 copy-start
  114.7 2.2 %copy.11 = bf16[256,1664]{1,0:T(8,128)(2,1)} copy(bf16[256,1664]{1,0:T(8,128)(2,1)} %bitcast.9) | data formatting | bytes 1703936
  116.9 0.0 copy-done
  116.9 0.9 copy.12
Async XLA Ops:
  114.7 2.2 %copy-start = (bf16[4,2,32,1664]{3,2,1,0:T(8,128)(2,1)S(1)}, bf16[4,2,32,1664]{3,2,1,0:T(8,128)(2,1)}, u32[]{:S(2)}) copy-start(bf16[4,2,32,1664]{3,2,1,0:T(8,128)(2,1)} %get-tuple-element.8) | copy-start | bytes 2555908

commit v4 on v3

--- a/solution.py
+++ b/solution.py
@@ -258,12 +258,12 @@
 
     for w in range(2):
         for d in range(2):
-            pass_on(w, d, 1, 0)
+            plan(4.0 * w, pass_on, w, d, 1, 0)
             for s in range(1, hops(w, d) + 1):
-                plan(2.3 * s + 0.5 * w, pass_on, w, d, 1, s)
-                plan((8.0, 9.0)[w] + 2.3 * s, pass_on, w, d, 0, s)
+                plan(2.3 * s + 4.1 * w, pass_on, w, d, 1, s)
+                plan((8.0, 12.5)[w] + 2.3 * s, pass_on, w, d, 0, s)
         plan(2.2, relay_act, w)
-        plan((8.0, 9.0)[w], arrive, w)
+        plan((8.0, 12.5)[w], arrive, w)
 
     order = [lax.rem(dp + o, NX) for o in (NX - 1, 1, 2, 0)]
     slots = ((0, 2, 1, 3), (1, 2, 0, 3))
@@ -314,7 +314,7 @@
                 x_next[d],
             )
 
-    starts = (18.5, 22.0)
+    starts = (18.5, 23.0)
     for w in range(2):
         plan(starts[w], gathered, w)
         for k in range(NX):
@@ -357,6 +357,34 @@
     run()
     for copy in sent:
         copy.wait_send()
+
+
+def settle_kernel(*refs):
+    ins, outs, bufs, (in_sem, out_sem) = refs[:3], refs[3:6], refs[6:9], refs[9:]
+    pieces = [(i, k) for k in range(NX) for i in range(3)]
+    arriving = []
+    for n, (i, k) in enumerate(pieces):
+        arriving.append(pltpu.make_async_copy(ins[i].at[k], bufs[i].at[k], in_sem.at[n]))
+        arriving[-1].start()
+    leaving = []
+    for n, (i, k) in enumerate(pieces):
+        arriving[n].wait()
+        leaving.append(pltpu.make_async_copy(bufs[i].at[k], outs[i].at[k], out_sem.at[n]))
+        leaving[-1].start()
+    for copy in leaving:
+        copy.wait()
+
+
+def settle(*arrays):
+    return pl.pallas_call(
+        settle_kernel,
+        out_shape=[jax.ShapeDtypeStruct(a.shape, a.dtype) for a in arrays],
+        in_specs=[pl.BlockSpec(memory_space=pl.ANY)] * 3,
+        out_specs=[pl.BlockSpec(memory_space=pl.ANY)] * 3,
+        scratch_shapes=[pltpu.VMEM(a.shape, a.dtype) for a in arrays]
+        + [pltpu.SemaphoreType.DMA((3 * NX,))] * 2,
+        name="settle",
+    )(*arrays)
 
 
 def main_call(tokens_t, hidden, gate_weight, up_weight):
@@ -414,7 +442,14 @@
         gate_weight.reshape(NC, part, width),
         up_weight.reshape(NC, part, width),
     )
-    return input_sum.T, gate_sum.reshape(features, width), up_sum.reshape(features, width)
+    gate_sum, up_sum, input_sum = settle(
+        gate_sum, up_sum, input_sum.reshape(NX, part // NX, tokens)
+    )
+    return (
+        input_sum.reshape(part, tokens).T,
+        gate_sum.reshape(features, width),
+        up_sum.reshape(features, width),
+    )
 
 
 def body(tokens, hidden_grad, gate_weight, up_weight):

time: 119 us -> 118 us (level); the launches traced: 118 us -> 118 us
  local copies, waits for them, and re-layouts: 4.57 us -> 0 us
  Pallas kernels: 113 us -> 117 us
    unnamed x5 -> x0, local copies, waits for them, and re-layouts: 4.57 us -> none
    pallas_call x0 -> x1, Pallas kernels: none -> 2.46 us  [settle(): pl.pallas_call(settle_kernel, out_shape=[jax.ShapeDtypeStruct(a.shape, a....]
    pallas_call x1, Pallas kernels: 113 us -> 115 us  [main_call(): pl.pallas_call(main_kernel, out_shape=[jax.ShapeDtypeStruct((NX, 2, half,...]
where the time goes in v4:
time: 118 us
  Pallas kernels  117 us (99%)
    pallas_call x1, Pallas kernels, main_call(): pl.pallas_call(main_kernel, out_shape=[jax.ShapeDtypeStruct((NX, 2, half,...  115 us
    pallas_call x1, Pallas kernels, settle(): pl.pallas_call(settle_kernel, out_shape=[jax.ShapeDtypeStruct(a.shape, a....  2.46 us

profile of v4, /device:TPU:1, one launch (start us, length us, event | category | flops | bytes accessed | tf_op | source)
XLA Modules:
  0.0 118.0 jit_solution(17169336100218387593)
XLA Ops:
  0.6 115.0 %main.1 = (bf16[4,2,32,1664]{3,2,1,0:T(8,128)(2,1)}, bf16[4,2,32,1664]{3,2,1,0:T(8,128)(2,1)}, bf16[64,512]{1,0:T(8,128)(2,1)}) custom-call(bf16[64,512]{1,0:T(8,128)(2,1)} %bitcast.11, bf16[16,1664]{1,0:T(8,128)(2,1)} %hidden_ref.1, bf16[4,64,1664]{2,1,0:T(8,128)(2,1)} %bitcast.9, bf16[4,64,1664]{2,1,0:T(8,128)(2,1)} %bitcast.10), custom_call_target="tpu_custom_call" | custom-call | tf_op jit(solution)/shard_map/main/pallas_call | solution.py:400
  115.6 2.5 %settle.1 = (bf16[4,2,32,1664]{3,2,1,0:T(8,128)(2,1)}, bf16[4,2,32,1664]{3,2,1,0:T(8,128)(2,1)}, bf16[4,16,512]{2,1,0:T(8,128)(2,1)}) custom-call(bf16[4,2,32,1664]{3,2,1,0:T(8,128)(2,1)} %get-tuple-element.9.refs_0_, bf16[4,2,32,1664]{3,2,1,0:T(8,128)(2,1)} %get-tuple-element.10.refs_1_, bf16[4,16,512]{2,1,0:T(8,128)(2,1)} %bitcast.12), custom_call_target="tpu_custom_call" | custom-call | tf_op jit(solution)/shard_map/settle/pallas_call | solution.py:379
